TPU v7x, 32 devices: a whole 2x2x4 slice. The times are simulated.
32 devices in a mesh: region: 2 (over y), member: 8 (over z, core), space: 2 (over x).
Axes of the slice: x: 2, y: 2, z: 4, core: 2. Of those that a mesh axis runs over, the one named last changes fastest.
Arguments:
- prior_trials: bfloat16 [80, 1536, 256], P('member', ('region', 'space')), parts along dimension 1, may hold values from -6 to 6
- prior_at_sensors: bfloat16 [80, 1536], P('member', ('region', 'space')), parts along dimension 1, may hold values from -6 to 6
- sensor_readings: bfloat16 [1536], P(('region', 'space')), parts along dimension 0, may hold values from -8 to 8
- sensor_noise_spread: bfloat16 [1536], P(('region', 'space')), parts along dimension 0, may hold values from 1 to 10
- nearby_readings: int32 [1536, 128], P(('region', 'space')), parts along dimension 0, may hold values from 0 to 1023, as said below
- subarea_cutoff_level: int32 [1536], P(('region', 'space')), parts along dimension 0, may hold values from 0 to 3
Outputs:
- analysis: bfloat16 [80, 1536, 256], P('member', ('region', 'space')), parts along dimension 1
There are 2 independent parts, one for each index of `region`. A program takes and returns all parts, laid end to end along the dimension named above; each array names one. Nothing has to cross between parts.
Inputs may be any that keep to these rules, and one draw needn't show every extreme that they name: `nearby_readings`: row c lists 128 distinct observations whose region-wide index o lies within (subarea_cutoff_level[c] + 2) * 64 of c and inside the region.
All inputs are finite; a program needn't handle non-finite values. Where the computation divides by a largest or mean magnitude, that divisor is 1e-20 or more.
Results may differ from a plain program's by a relative error of at most 0.0053.
Values may be sent and summed in bfloat16 or wider, within the bound.
A program may use at most 64 MiB of HBM per device.

v0:
```python
import jax
import jax.numpy as jnp
from jax import lax
from jax.sharding import PartitionSpec as P

NS_STEPS = 4


def padded(value, sides, width):
    for axis, dim in sides:
        count, length = (lax.axis_size(axis), value.shape[dim])
        up = [(i, (i + 1) % count) for i in range(count - 1)]
        down = [(j, i) for i, j in up]
        last = lax.slice_in_dim(value, length - width, length, axis=dim)
        leading = lax.slice_in_dim(value, 0, width, axis=dim)
        before = lax.ppermute(last, axis, up)
        after = lax.ppermute(leading, axis, down)
        value = jnp.concatenate([before, value, after], axis=dim)
    return value


def prepare(picked, trial_lines, offsets, tier_ids, obs_count):
    observ = picked[:trial_lines]
    ens_mean = jnp.mean(observ, axis=0)
    anomaly = observ - ens_mean
    innovation = picked[trial_lines] - ens_mean
    radius = (tier_ids.astype(jnp.float32) + 2.0) * (0.5 * obs_count)
    distance = jnp.abs(offsets).astype(jnp.float32) / radius[:, None]
    weight = jnp.exp(-2.0 * distance * distance) / picked[trial_lines + 1]
    return (anomaly, innovation, weight)


def spread_terms(anomaly, innovation, weight, trial_lines):
    fit_sum = jnp.sum(weight * innovation * innovation)
    spread = jnp.sum(weight * jnp.sum(anomaly * anomaly, axis=0)) / (trial_lines - 1.0)
    return (fit_sum, spread)


def transform(anomaly, innovation, weight, inflation, trial_lines, sweeps):
    exact = lax.Precision.HIGHEST
    weighted = anomaly * weight[None]
    gram = jnp.einsum("ank,bnk->abn", weighted, anomaly, precision=exact)
    identity = jnp.eye(trial_lines, dtype=jnp.float32)[:, :, None]
    matrix = gram + (trial_lines - 1.0) / inflation * identity
    row_bound = jnp.max(jnp.sum(jnp.abs(matrix), axis=1), axis=0)
    root_iter = matrix / row_bound
    inverse = jnp.broadcast_to(identity, matrix.shape)
    for repeat in range(sweeps):
        factor = 1.5 * identity - 0.5 * jnp.einsum(
            "abn,bcn->acn", inverse, root_iter, precision=exact
        )
        root_iter = jnp.einsum("abn,bcn->acn", root_iter, factor, precision=exact)
        inverse = jnp.einsum("abn,bcn->acn", factor, inverse, precision=exact)
    inv_root = inverse / jnp.sqrt(row_bound)
    target = jnp.sum(weighted * innovation[None], axis=2)
    half_gain = jnp.einsum("abn,bn->an", inv_root, target, precision=exact)
    mean_gain = jnp.einsum("abn,bn->an", inv_root, half_gain, precision=exact)
    weights_full = jnp.sqrt(trial_lines - 1.0) * inv_root + mean_gain[:, None, :]
    centred = weights_full - jnp.mean(weights_full, axis=0, keepdims=True) + 1.0 / trial_lines
    return centred.astype(jnp.bfloat16)


def select_domains(window, trial_lines, obs_lists, col_ids, tier_ids, halo_cells):
    row_count = window.shape[0]
    dom_count, obs_count = obs_lists.shape
    picked = jnp.take(window, obs_lists.reshape(-1), axis=1).reshape(
        row_count, dom_count, obs_count
    )
    picked = picked.astype(jnp.float32)
    offsets = obs_lists - (col_ids + halo_cells)[:, None]
    return prepare(picked, trial_lines, offsets, tier_ids, obs_count)


def per_device(
    prior_trials,
    prior_at_sensors,
    sensor_readings,
    sensor_noise_spread,
    nearby_readings,
    subarea_cutoff_level,
):
    patch_cells = prior_trials.shape[1]
    obs_count = nearby_readings.shape[1]
    halo_cells = 5 * obs_count // 2
    groups = lax.axis_size("member")
    domains = patch_cells // groups
    obs_rows = jnp.stack([sensor_readings, sensor_noise_spread], axis=0)
    gathered = lax.all_gather(prior_at_sensors, "member", axis=0, tiled=True)
    window = padded(jnp.concatenate([gathered, obs_rows], axis=0), (("space", 1),), halo_cells)
    trial_lines = window.shape[0] - 2
    first_col = lax.axis_index("member") * domains
    own_lists = lax.dynamic_slice_in_dim(nearby_readings, first_col, domains, 0)
    own_tiers = lax.dynamic_slice_in_dim(subarea_cutoff_level, first_col, domains, 0)
    own_columns = first_col + jnp.arange(domains, dtype=jnp.int32)
    anomaly, innovation, weight = select_domains(
        window, trial_lines, own_lists, own_columns, own_tiers, halo_cells
    )
    fit_sum, spread = spread_terms(anomaly, innovation, weight, trial_lines)
    fit_sum, spread = lax.psum((fit_sum, spread), ("member", "space"))
    inflation = fit_sum / spread
    trans_w = transform(anomaly, innovation, weight, inflation, trial_lines, NS_STEPS)
    incoming_pieces = lax.all_to_all(
        prior_trials, "member", split_axis=1, concat_axis=0, tiled=True
    )
    updated = jnp.einsum(
        "inc,ijn->jnc", incoming_pieces, trans_w, preferred_element_type=jnp.float32
    ).astype(jnp.bfloat16)
    return lax.all_to_all(updated, "member", split_axis=0, concat_axis=1, tiled=True)


def solution(mesh):
    return jax.shard_map(
        per_device,
        mesh=mesh,
        in_specs=(
            P("member", ("region", "space"), None),
            P("member", ("region", "space")),
            P(("region", "space")),
            P(("region", "space")),
            P(("region", "space"), None),
            P(("region", "space")),
        ),
        out_specs=P("member", ("region", "space"), None),
        check_vma=False,
    )
```

profile of v0, /device:TPU:0, one launch (start us, length us, event | category | flops | bytes accessed | tf_op | source)
XLA Modules:
  0.0 223.0 jit_solution(4702585472627936783)
XLA Ops:
  0.0 15.8 %all-gather = bf16[8,10,384]{2,1,0:T(8,128)(2,1)S(1)} all-gather(bf16[1,10,384]{2,1,0:T(8,128)(2,1)} %bitcast.124), channel_id=1, replica_groups=mesh['region'=2,'member'=8,'space'=2] {'member'}, dimensions={0}, use_global_device_ids=true | all-gather | bytes 69120 | tf_op jit(solution)/shard_map/all_gather | solution.py:88
  16.0 0.8 stack.8
  16.8 0.8 stack.9
  17.7 3.4 %collective-permute-start = (bf16[82,320]{0,1:T(8,128)(2,1)S(1)}, bf16[82,320]{0,1:T(8,128)(2,1)S(1)}, u32[]{:S(2)}, u32[]{:S(2)}) collective-permute-start(bf16[82,320]{0,1:T(8,128)(2,1)S(1)} %get-tuple-element.14), channel_id=1, source_target_pairs={{0,1},{2,3},{4,5},{6,7},{8,9},{10,11},{12,13},{14,15},{16,17},{18,... | collective-permute-start | bytes 157448 | tf_op jit(solution)/shard_map/ppermute | solution.py:16
  21.1 1.3 collective-permute-start.1
  22.4 4.5 %copy.84 = bf16[10,384,256]{2,0,1:T(8,128)(2,1)} copy(bf16[10,384,256]{2,1,0:T(8,128)(2,1)} %param.6) | data formatting | bytes 3932160 | tf_op args[0]
  26.9 4.7 %all-to-all-start = ((bf16[10,384,256]{2,0,1:T(8,128)(2,1)}), bf16[10,384,256]{2,0,1:T(8,128)(2,1)}, u32[]{:S(2)}, u32[]{:S(2)}) async-start(bf16[10,384,256]{2,0,1:T(8,128)(2,1)} %copy.84), calls=%async_computation | async-start | bytes 6291456 | tf_op jit(solution)/shard_map/all_to_all | solution.py:102
  31.6 0.8 compare_and_fusion
  32.4 0.8 add_multiply_fusion
  33.3 18.1 %gather_fusion = bf16[6144,82]{1,0:T(8,128)(2,1)S(1)} fusion(bf16[82,1024]{0,1:T(8,128)(2,1)S(1)} %pad_maximum_fusion, s32[6144]{0:T(1024)S(1)} %broadcast_clamp_fusion), kind=kCustom, calls=%fused_computation | custom fusion | bytes 2039808 | tf_op jit(solution)/shard_map/jit(_take)/gather | solution.py:66
  51.4 0.9 copy.69
  52.8 1.8 multiply_reduce_fusion
  56.0 56.4 %all-reduce = (f32[]{:T(128)}, f32[]{:T(128)}) all-reduce(f32[]{:T(128)S(6)} %div.56, f32[]{:T(128)} %get-tuple-element.5), channel_id=1, replica_groups=mesh['region'=2,'member'=8,'space'=2] {'member','space'}, use_global_device_ids=true, to_apply=%region_3.4 | all-reduce | flops 2 | bytes 16 | tf_op jit(solution)/shard_map/psum | solution.py:99
  113.7 7.0 %abs_reduce_fusion = (f32[80,48]{0,1:T(8,128)S(1)}, f32[48,80,80]{2,1,0:T(8,128)}) fusion(f32[80,80]{0,1:T(8,128)S(1)} %fusion.65, f32[80,48,128]{2,1,0:T(8,128)} %get-tuple-element.10, f32[80,48,128]{2,1,0:T(8,128)S(1)} %get-tuple-element.11), kind=kOutput, calls=%fused_computation.40 | convolution fusion | flops 472776960 | bytes 5201920 | tf_op jit(solution)/shard_map/ank,bnk->abn/dot_general | solution.py:42
  120.8 3.6 %fusion.61 = f32[48,80,80]{2,1,0:T(8,128)S(1)} fusion(f32[80,80]{0,1:T(8,128)S(1)} %fusion.67, f32[48,80,80]{2,1,0:T(8,128)} %get-tuple-element.17, f32[48]{0:T(128)S(1)} %reduce_max.9, f32[80,80]{0,1:T(8,128)S(1)} %fusion.65), kind=kOutput, calls=%fused_computation.71 | convolution fusion | flops 295526400 | bytes 2508992 | tf_op jit(solution)/shard_map/abn,bcn->acn/dot_general | solution.py:49
  124.4 1.8 fusion.34
  126.2 2.4 %fusion.33 = f32[48,80,80]{2,1,0:T(8,128)S(1)} fusion(f32[48,80,80]{2,1,0:T(8,128)S(1)} %fusion.61, f32[80,80]{0,1:T(8,128)S(1)} %fusion.66, f32[48,80,80]{2,1,0:T(8,128)S(1)} %copy-done.2, f32[48]{0:T(128)S(1)} %reduce_max.9, f32[80,80]{0,1:T(8,128)S(1)} %fusion.65), kind=kOutput, calls=%fused_computation.45 | convolution fusion | flops 296140800 | bytes 3737792 | tf_op jit(solution)/shard_map/abn,bcn->acn/dot_general | solution.py:52
  128.6 2.4 %fusion.19 = f32[48,80,80]{2,1,0:T(8,128)S(1)} fusion(f32[48,80,80]{2,1,0:T(8,128)S(1)} %fusion.33, f32[48,80,80]{2,1,0:T(8,128)S(1)} %fusion.34), kind=kOutput, calls=%fused_computation.24 | convolution fusion | flops 294912000 | bytes 3686400 | tf_op jit(solution)/shard_map/abn,bcn->acn/dot_general | solution.py:49
  131.1 2.2 fusion.21
  133.3 4.3 %fusion.17 = f32[48,80,80]{2,1,0:T(8,128)S(1)} fusion(f32[48,80,80]{2,1,0:T(8,128)} %copy-done.1, f32[48,80,80]{2,1,0:T(8,128)} %copy-done, f32[80,80]{0,1:T(8,128)S(1)} %fusion.66), kind=kOutput, calls=%fused_computation.22 | convolution fusion | flops 295526400 | bytes 3712000 | tf_op jit(solution)/shard_map/abn,bcn->acn/dot_general | solution.py:52
  137.7 2.2 fusion.12
  139.9 2.3 %fusion.14 = f32[48,80,80]{2,1,0:T(8,128)S(1)} fusion(f32[48,80,80]{2,1,0:T(8,128)S(1)} %fusion.21, f32[48,80,80]{2,1,0:T(8,128)S(1)} %fusion.12, f32[80,80]{0,1:T(8,128)S(1)} %fusion.66), kind=kOutput, calls=%fused_computation.18 | convolution fusion | flops 295526400 | bytes 3712000 | tf_op jit(solution)/shard_map/abn,bcn->acn/dot_general | solution.py:53
  142.1 2.5 %fusion.10 = f32[48,80,80]{2,1,0:T(8,128)S(1)} fusion(f32[48,80,80]{2,1,0:T(8,128)S(1)} %fusion.17, f32[48,80,80]{2,1,0:T(8,128)S(1)} %fusion.12, f32[80,80]{0,1:T(8,128)S(1)} %fusion.66), kind=kOutput, calls=%fused_computation.14 | convolution fusion | flops 295526400 | bytes 3712000 | tf_op jit(solution)/shard_map/abn,bcn->acn/dot_general | solution.py:52
  144.7 2.2 fusion.6
  146.9 3.5 %fusion.36 = f32[48,80,80]{1,2,0:T(8,128)S(1)} fusion(f32[48,80,80]{2,1,0:T(8,128)S(1)} %fusion.6, f32[48,80,80]{2,1,0:T(8,128)S(1)} %fusion.14, f32[48]{0:T(128)S(1)} %sqrt.7, f32[80,80]{0,1:T(8,128)S(1)} %fusion.66), kind=kOutput, calls=%fused_computation.48 | convolution fusion | flops 295833600 | bytes 3712192 | tf_op jit(solution)/shard_map/abn,bcn->acn/dot_general | solution.py:53
  150.4 3.2 %fusion.39 = f32[80,48,1]{0,2,1:T(1,128)S(1)} fusion(f32[80,48,1]{0,2,1:T(1,128)S(1)} %copy.103, f32[48,80,80]{1,2,0:T(8,128)S(1)} %fusion.36), kind=kOutput, calls=%fused_computation.49 | convolution fusion | flops 3686400 | bytes 1259520 | tf_op jit(solution)/shard_map/abn,bn->an/dot_general | solution.py:56
  153.5 3.2 %fusion = f32[48,1,80]{2,1,0:T(1,128)S(1)} fusion(f32[80,48,1]{0,2,1:T(1,128)S(1)} %fusion.39, f32[48,80,80]{1,2,0:T(8,128)S(1)} %fusion.36), kind=kOutput, calls=%fused_computation.1 | convolution fusion | flops 3686400 | bytes 1259520 | tf_op jit(solution)/shard_map/abn,bn->an/dot_general | solution.py:57
  157.3 2.6 %copy.86 = bf16[8,10,48,256]{3,2,1,0:T(8,128)(2,1)S(1)} copy(bf16[8,10,48,256]{3,1,2,0:T(8,128)(2,1)} %bitcast.32) | data formatting | bytes 3932160 | tf_op jit(solution)/shard_map/all_to_all | solution.py:102
  160.0 2.3 %convert_bitcast_fusion = bf16[80,48,256]{2,0,1:T(8,128)(2,1)S(1)} fusion(bf16[80,48,256]{2,1,0:T(8,128)(2,1)S(1)} %bitcast.116, f32[48,80,80]{1,2,0:T(8,128)S(1)} %fusion.36, f32[80,48]{0,1:T(8,128)S(1)} %broadcast_multiply_fusion.1, f32[80,48]{0,1:T(8,128)S(1)} %bitcast.120), kind=kOutput, calls=%fused_computation.36 | convolution fusion | flops 159805440 | bytes 5191680 | tf_op jit(solution)/shard_map/inc,ijn->jnc/dot_general | solution.py:105
  162.3 0.7 copy.89
  162.9 58.4 %all_to_all.36 = bf16[80,48,256]{2,1,0:T(8,128)(2,1)S(1)} all-to-all(bf16[80,48,256]{2,1,0:T(8,128)(2,1)S(1)} %copy.89), channel_id=1, replica_groups=mesh['region'=2,'member'=8,'space'=2] {'member'}, dimensions={0} | all-to-all | bytes 3932160 | tf_op jit(solution)/shard_map/all_to_all | solution.py:108
  221.3 1.5 copy.90
  (31 shorter events, 2.5 us)
Async XLA Ops:
  17.7 15.5 %collective-permute-start = (bf16[82,320]{0,1:T(8,128)(2,1)S(1)}, bf16[82,320]{0,1:T(8,128)(2,1)S(1)}, u32[]{:S(2)}, u32[]{:S(2)}) collective-permute-start(bf16[82,320]{0,1:T(8,128)(2,1)S(1)} %get-tuple-element.14), channel_id=1, source_target_pairs={{0,1},{2,3},{4,5},{6,7},{8,9},{10,11},{12,13},{14,15},{16,17},{18,... | collective-permute-start | bytes 157448 | tf_op jit(solution)/shard_map/ppermute | solution.py:16
  21.1 12.1 %collective-permute-start.1 = (bf16[82,320]{0,1:T(8,128)(2,1)S(1)}, bf16[82,320]{0,1:T(8,128)(2,1)S(1)}, u32[]{:S(2)}, u32[]{:S(2)}) collective-permute-start(bf16[82,320]{0,1:T(8,128)(2,1)S(1)} %get-tuple-element.15), channel_id=1, source_target_pairs={{1,0},{3,2},{5,4},{7,6},{9,8},{11,10},{13,12},{15,14},{17,16},{19,... | collective-permute-start | bytes 157448 | tf_op jit(solution)/shard_map/ppermute | solution.py:17
  26.9 130.4 %all-to-all-start = ((bf16[10,384,256]{2,0,1:T(8,128)(2,1)}), bf16[10,384,256]{2,0,1:T(8,128)(2,1)}, u32[]{:S(2)}, u32[]{:S(2)}) async-start(bf16[10,384,256]{2,0,1:T(8,128)(2,1)} %copy.84), calls=%async_computation | async-start | bytes 6291456 | tf_op jit(solution)/shard_map/all_to_all | solution.py:102
  124.4 1.8 copy-start.2
  128.6 2.4 %copy-start.1 = (f32[48,80,80]{2,1,0:T(8,128)}, f32[48,80,80]{2,1,0:T(8,128)S(1)}, u32[]{:S(2)}) copy-start(f32[48,80,80]{2,1,0:T(8,128)S(1)} %fusion.33) | copy-start | bytes 3686404
  131.0 2.2 copy-start
where the time goes:
time: 227 us; the launch traced here: 223 us
  blocking collectives  131 us (58%)
  matrix products  45 us (20%)
  local copies, waits for them, and re-layouts  30.1 us (13%)
  starting transfers between devices  9.35 us (4%)
  other arithmetic  5.51 us (2%)
  between operations  2.5 us (1%)
    all_to_all x1, blocking collectives, per_device(): lax.all_to_all(updated, 'member', split_axis=0, concat_axis=1, tiled=True)  58.4 us
    psum x1, blocking collectives, per_device(): fit_sum, spread = lax.psum((fit_sum, spread), ('member', 'space'))  56.4 us
    gather x2, local copies, waits for them, and re-layouts, select_domains(): jnp.take(window, obs_lists.reshape(-1), axis=1)  19 us
    all_gather x1, blocking collectives, per_device(): gathered = lax.all_gather(prior_at_sensors, 'member', axis=0, tiled=True)  15.8 us
    dot_general x4, matrix products, transform(): jnp.einsum('abn,bcn->acn', inverse, root_iter, precision=exact)  10.4 us
    dot_general x4, matrix products, transform(): inverse = jnp.einsum('abn,bcn->acn', factor, inverse, precision=exact)  9.78 us
    dot_general x3, matrix products, transform(): root_iter = jnp.einsum('abn,bcn->acn', root_iter, factor, precision=exact)  9.26 us
    dot_general x1, matrix products, transform(): gram = jnp.einsum('ank,bnk->abn', weighted, anomaly, precision=exact)  7.01 us
  transfers between devices with their start and end apart: 3, of which 0 were waited for; matrix products, arithmetic and copies ran while one was open for 32% of the time, Pallas kernels for 0%

commit v1 on v0

--- a/solution.py
+++ b/solution.py
@@ -105,7 +105,12 @@
     updated = jnp.einsum(
         "inc,ijn->jnc", incoming_pieces, trans_w, preferred_element_type=jnp.float32
     ).astype(jnp.bfloat16)
-    return lax.all_to_all(updated, "member", split_axis=0, concat_axis=1, tiled=True)
+    return jnp.concatenate(
+        lax.all_to_all(
+            jnp.stack(jnp.split(updated, lax.axis_size("member"), axis=0)), "member", 0, 0
+        ),
+        axis=1,
+    )
 
 
 def solution(mesh):

time: 227 us -> 229 us (level)
    unnamed x9 -> x16, local copies, waits for them, and re-layouts: 4.63 us -> 5.38 us
where the time goes in v1:
time: 229 us; the launch traced here: 224 us
  blocking collectives  131 us (57%)
  matrix products  45 us (20%)
  local copies, waits for them, and re-layouts  31.3 us (14%)
  starting transfers between devices  9.35 us (4%)
  other arithmetic  5.51 us (2%)
  between operations  2.59 us (1%)
    all_to_all x1, blocking collectives, per_device(): lax.all_to_all(jnp.stack(jnp.split(updated, lax.axis_size('member'), axis...  58.4 us
    psum x1, blocking collectives, per_device(): fit_sum, spread = lax.psum((fit_sum, spread), ('member', 'space'))  56.4 us
    gather x2, local copies, waits for them, and re-layouts, select_domains(): jnp.take(window, obs_lists.reshape(-1), axis=1)  19 us
    all_gather x1, blocking collectives, per_device(): gathered = lax.all_gather(prior_at_sensors, 'member', axis=0, tiled=True)  15.8 us
    dot_general x4, matrix products, transform(): jnp.einsum('abn,bcn->acn', inverse, root_iter, precision=exact)  10.4 us
    dot_general x4, matrix products, transform(): inverse = jnp.einsum('abn,bcn->acn', factor, inverse, precision=exact)  9.78 us
    dot_general x3, matrix products, transform(): root_iter = jnp.einsum('abn,bcn->acn', root_iter, factor, precision=exact)  9.26 us
    dot_general x1, matrix products, transform(): gram = jnp.einsum('ank,bnk->abn', weighted, anomaly, precision=exact)  7.01 us
  transfers between devices with their start and end apart: 3, of which 0 were waited for; matrix products, arithmetic and copies ran while one was open for 32% of the time, Pallas kernels for 0%

profile of v1, /device:TPU:0, one launch (start us, length us, event | category | flops | bytes accessed | tf_op | source)
XLA Modules:
  0.0 224.3 jit_solution(8232275140895990626)
XLA Ops:
  0.0 15.8 %all-gather = bf16[8,10,384]{2,1,0:T(8,128)(2,1)S(1)} all-gather(bf16[1,10,384]{2,1,0:T(8,128)(2,1)} %bitcast.154), channel_id=1, replica_groups=mesh['region'=2,'member'=8,'space'=2] {'member'}, dimensions={0}, use_global_device_ids=true | all-gather | bytes 69120 | tf_op jit(solution)/shard_map/all_gather | solution.py:88
  16.0 0.8 stack.44
  16.8 0.8 stack.45
  17.7 3.4 %collective-permute-start = (bf16[82,320]{0,1:T(8,128)(2,1)S(1)}, bf16[82,320]{0,1:T(8,128)(2,1)S(1)}, u32[]{:S(2)}, u32[]{:S(2)}) collective-permute-start(bf16[82,320]{0,1:T(8,128)(2,1)S(1)} %get-tuple-element.14), channel_id=1, source_target_pairs={{0,1},{2,3},{4,5},{6,7},{8,9},{10,11},{12,13},{14,15},{16,17},{18,... | collective-permute-start | bytes 157448 | tf_op jit(solution)/shard_map/ppermute | solution.py:16
  21.1 1.3 collective-permute-start.1
  22.4 4.5 %copy.107 = bf16[10,384,256]{2,0,1:T(8,128)(2,1)} copy(bf16[10,384,256]{2,1,0:T(8,128)(2,1)} %param.6) | data formatting | bytes 3932160 | tf_op args[0]
  26.9 4.7 %all-to-all-start = ((bf16[10,384,256]{2,0,1:T(8,128)(2,1)}), bf16[10,384,256]{2,0,1:T(8,128)(2,1)}, u32[]{:S(2)}, u32[]{:S(2)}) async-start(bf16[10,384,256]{2,0,1:T(8,128)(2,1)} %copy.107), calls=%async_computation | async-start | bytes 6291456 | tf_op jit(solution)/shard_map/all_to_all | solution.py:102
  31.6 0.8 compare_and_fusion
  32.4 0.8 add_multiply_fusion
  33.3 18.1 %gather_fusion = bf16[6144,82]{1,0:T(8,128)(2,1)S(1)} fusion(bf16[82,1024]{0,1:T(8,128)(2,1)S(1)} %pad_maximum_fusion, s32[6144]{0:T(1024)S(1)} %broadcast_clamp_fusion), kind=kCustom, calls=%fused_computation | custom fusion | bytes 2039808 | tf_op jit(solution)/shard_map/jit(_take)/gather | solution.py:66
  51.4 0.9 copy.92
  52.8 1.8 multiply_reduce_fusion
  56.0 56.4 %all-reduce = (f32[]{:T(128)}, f32[]{:T(128)}) all-reduce(f32[]{:T(128)S(6)} %div.56, f32[]{:T(128)} %get-tuple-element.5), channel_id=1, replica_groups=mesh['region'=2,'member'=8,'space'=2] {'member','space'}, use_global_device_ids=true, to_apply=%region_3.4 | all-reduce | flops 2 | bytes 16 | tf_op jit(solution)/shard_map/psum | solution.py:99
  113.7 7.0 %abs_reduce_fusion = (f32[80,48]{0,1:T(8,128)S(1)}, f32[48,80,80]{2,1,0:T(8,128)}) fusion(f32[80,80]{0,1:T(8,128)S(1)} %fusion.73, f32[80,48,128]{2,1,0:T(8,128)} %get-tuple-element.10, f32[80,48,128]{2,1,0:T(8,128)S(1)} %get-tuple-element.11), kind=kOutput, calls=%fused_computation.40 | convolution fusion | flops 472776960 | bytes 5201920 | tf_op jit(solution)/shard_map/ank,bnk->abn/dot_general | solution.py:42
  120.8 3.6 %fusion.61 = f32[48,80,80]{2,1,0:T(8,128)S(1)} fusion(f32[80,80]{0,1:T(8,128)S(1)} %fusion.75, f32[48,80,80]{2,1,0:T(8,128)} %get-tuple-element.17, f32[48]{0:T(128)S(1)} %reduce_max.9, f32[80,80]{0,1:T(8,128)S(1)} %fusion.73), kind=kOutput, calls=%fused_computation.71 | convolution fusion | flops 295526400 | bytes 2508992 | tf_op jit(solution)/shard_map/abn,bcn->acn/dot_general | solution.py:49
  124.4 1.8 fusion.34
  126.2 2.4 %fusion.33 = f32[48,80,80]{2,1,0:T(8,128)S(1)} fusion(f32[48,80,80]{2,1,0:T(8,128)S(1)} %fusion.61, f32[80,80]{0,1:T(8,128)S(1)} %fusion.74, f32[48,80,80]{2,1,0:T(8,128)S(1)} %copy-done.2, f32[48]{0:T(128)S(1)} %reduce_max.9, f32[80,80]{0,1:T(8,128)S(1)} %fusion.73), kind=kOutput, calls=%fused_computation.45 | convolution fusion | flops 296140800 | bytes 3737792 | tf_op jit(solution)/shard_map/abn,bcn->acn/dot_general | solution.py:52
  128.6 2.4 %fusion.19 = f32[48,80,80]{2,1,0:T(8,128)S(1)} fusion(f32[48,80,80]{2,1,0:T(8,128)S(1)} %fusion.33, f32[48,80,80]{2,1,0:T(8,128)S(1)} %fusion.34), kind=kOutput, calls=%fused_computation.24 | convolution fusion | flops 294912000 | bytes 3686400 | tf_op jit(solution)/shard_map/abn,bcn->acn/dot_general | solution.py:49
  131.0 2.2 fusion.21
  133.3 4.3 %fusion.17 = f32[48,80,80]{2,1,0:T(8,128)S(1)} fusion(f32[48,80,80]{2,1,0:T(8,128)} %copy-done.1, f32[48,80,80]{2,1,0:T(8,128)} %copy-done, f32[80,80]{0,1:T(8,128)S(1)} %fusion.74), kind=kOutput, calls=%fused_computation.22 | convolution fusion | flops 295526400 | bytes 3712000 | tf_op jit(solution)/shard_map/abn,bcn->acn/dot_general | solution.py:52
  137.7 2.2 fusion.12
  139.8 2.3 %fusion.14 = f32[48,80,80]{2,1,0:T(8,128)S(1)} fusion(f32[48,80,80]{2,1,0:T(8,128)S(1)} %fusion.21, f32[48,80,80]{2,1,0:T(8,128)S(1)} %fusion.12, f32[80,80]{0,1:T(8,128)S(1)} %fusion.74), kind=kOutput, calls=%fused_computation.18 | convolution fusion | flops 295526400 | bytes 3712000 | tf_op jit(solution)/shard_map/abn,bcn->acn/dot_general | solution.py:53
  142.1 2.5 %fusion.10 = f32[48,80,80]{2,1,0:T(8,128)S(1)} fusion(f32[48,80,80]{2,1,0:T(8,128)S(1)} %fusion.17, f32[48,80,80]{2,1,0:T(8,128)S(1)} %fusion.12, f32[80,80]{0,1:T(8,128)S(1)} %fusion.74), kind=kOutput, calls=%fused_computation.14 | convolution fusion | flops 295526400 | bytes 3712000 | tf_op jit(solution)/shard_map/abn,bcn->acn/dot_general | solution.py:52
  144.7 2.2 fusion.6
  146.9 3.5 %fusion.36 = f32[48,80,80]{1,2,0:T(8,128)S(1)} fusion(f32[48,80,80]{2,1,0:T(8,128)S(1)} %fusion.6, f32[48,80,80]{2,1,0:T(8,128)S(1)} %fusion.14, f32[48]{0:T(128)S(1)} %sqrt.7, f32[80,80]{0,1:T(8,128)S(1)} %fusion.74), kind=kOutput, calls=%fused_computation.48 | convolution fusion | flops 295833600 | bytes 3712192 | tf_op jit(solution)/shard_map/abn,bcn->acn/dot_general | solution.py:53
  150.4 3.2 %fusion.39 = f32[80,48,1]{0,2,1:T(1,128)S(1)} fusion(f32[80,48,1]{0,2,1:T(1,128)S(1)} %copy.126, f32[48,80,80]{1,2,0:T(8,128)S(1)} %fusion.36), kind=kOutput, calls=%fused_computation.49 | convolution fusion | flops 3686400 | bytes 1259520 | tf_op jit(solution)/shard_map/abn,bn->an/dot_general | solution.py:56
  153.5 3.2 %fusion = f32[48,1,80]{2,1,0:T(1,128)S(1)} fusion(f32[80,48,1]{0,2,1:T(1,128)S(1)} %fusion.39, f32[48,80,80]{1,2,0:T(8,128)S(1)} %fusion.36), kind=kOutput, calls=%fused_computation.1 | convolution fusion | flops 3686400 | bytes 1259520 | tf_op jit(solution)/shard_map/abn,bn->an/dot_general | solution.py:57
  157.3 2.9 %copy.109 = bf16[8,10,48,256]{3,2,1,0:T(8,128)(2,1)S(1)} copy(bf16[8,10,48,256]{3,1,2,0:T(8,128)(2,1)} %bitcast.32) | data formatting | bytes 3932160 | tf_op jit(solution)/shard_map/all_to_all | solution.py:102
  160.2 2.3 %convert_bitcast_fusion = bf16[80,48,256]{2,0,1:T(8,128)(2,1)S(1)} fusion(bf16[80,48,256]{2,1,0:T(8,128)(2,1)S(1)} %bitcast.147, f32[48,80,80]{1,2,0:T(8,128)S(1)} %fusion.36, f32[80,48]{0,1:T(8,128)S(1)} %broadcast_multiply_fusion.1, f32[80,48]{0,1:T(8,128)S(1)} %bitcast.150), kind=kOutput, calls=%fused_computation.36 | convolution fusion | flops 159805440 | bytes 5191680 | tf_op jit(solution)/shard_map/inc,ijn->jnc/dot_general | solution.py:105
  163.4 0.8 copy.112
  164.2 58.4 %all_to_all.23 = bf16[8,10,48,256]{3,2,1,0:T(8,128)(2,1)S(1)} all-to-all(bf16[8,10,48,256]{3,2,1,0:T(8,128)(2,1)S(1)} %copy.112), channel_id=1, replica_groups=mesh['region'=2,'member'=8,'space'=2] {'member'}, dimensions={0} | all-to-all | bytes 3932160 | tf_op jit(solution)/shard_map/all_to_all | solution.py:109
  222.6 1.5 copy.113
  (39 shorter events, 3.4 us)
Async XLA Ops:
  17.7 15.5 %collective-permute-start = (bf16[82,320]{0,1:T(8,128)(2,1)S(1)}, bf16[82,320]{0,1:T(8,128)(2,1)S(1)}, u32[]{:S(2)}, u32[]{:S(2)}) collective-permute-start(bf16[82,320]{0,1:T(8,128)(2,1)S(1)} %get-tuple-element.14), channel_id=1, source_target_pairs={{0,1},{2,3},{4,5},{6,7},{8,9},{10,11},{12,13},{14,15},{16,17},{18,... | collective-permute-start | bytes 157448 | tf_op jit(solution)/shard_map/ppermute | solution.py:16
  21.1 12.1 %collective-permute-start.1 = (bf16[82,320]{0,1:T(8,128)(2,1)S(1)}, bf16[82,320]{0,1:T(8,128)(2,1)S(1)}, u32[]{:S(2)}, u32[]{:S(2)}) collective-permute-start(bf16[82,320]{0,1:T(8,128)(2,1)S(1)} %get-tuple-element.15), channel_id=1, source_target_pairs={{1,0},{3,2},{5,4},{7,6},{9,8},{11,10},{13,12},{15,14},{17,16},{19,... | collective-permute-start | bytes 157448 | tf_op jit(solution)/shard_map/ppermute | solution.py:17
  26.9 130.4 %all-to-all-start = ((bf16[10,384,256]{2,0,1:T(8,128)(2,1)}), bf16[10,384,256]{2,0,1:T(8,128)(2,1)}, u32[]{:S(2)}, u32[]{:S(2)}) async-start(bf16[10,384,256]{2,0,1:T(8,128)(2,1)} %copy.107), calls=%async_computation | async-start | bytes 6291456 | tf_op jit(solution)/shard_map/all_to_all | solution.py:102
  124.4 1.8 copy-start.2
  128.6 2.4 %copy-start.1 = (f32[48,80,80]{2,1,0:T(8,128)}, f32[48,80,80]{2,1,0:T(8,128)S(1)}, u32[]{:S(2)}) copy-start(f32[48,80,80]{2,1,0:T(8,128)S(1)} %fusion.33) | copy-start | bytes 3686404
  131.0 2.2 copy-start
